TPU v7x, 32 devices: a whole 2x2x4 slice. The times are simulated.
32 devices in a mesh: loop: 4 (over y, x), bulk: 8 (over z, core).
Axes of the slice: x: 2, y: 2, z: 4, core: 2. Of those that a mesh axis runs over, the one named last changes fastest.
Arguments:
- series: float32 [4224, 3072], P('loop', 'bulk'), may hold values from -64 to 64
Outputs:
- correlation: float32 [4, 1056, 4224], P(None, 'bulk', 'loop')
All inputs are finite; a program needn't handle non-finite values.
Results may differ from a plain program's by a relative error of at most 0.0011.
Values may be sent and summed in bfloat16 or wider, within the bound.
A program may use at most 64 MiB of HBM per device.

v0:
```python
import jax
import jax.numpy as jnp
from jax import lax
from jax.sharding import PartitionSpec as P

TIME = 3072


epsilon = 1e-06


def normalize(centered, square_total):
    return (centered * lax.rsqrt(square_total / TIME + epsilon)).astype(jnp.bfloat16)


def contract(first_operand, second_operand):
    product = lax.dot_general(
        first_operand, second_operand, (((1,), (1,)), ((), ())), preferred_element_type=jnp.float32
    )
    return product / TIME


def cycle_gather(own_rows):
    return lax.all_gather(own_rows, "loop", axis=0, tiled=True)


def on_device(series):
    share_rows = series.shape[0] // lax.axis_size("bulk")
    average = lax.psum(jnp.sum(series, axis=1, keepdims=True), "bulk") / TIME
    centered = series - average
    squares = lax.psum(jnp.sum(centered * centered, axis=1, keepdims=True), "bulk")
    zscore = normalize(centered, squares)
    row_series = lax.all_gather(zscore, "bulk", axis=1, tiled=True)
    own_rows = lax.dynamic_slice_in_dim(
        row_series, lax.axis_index("bulk") * share_rows, share_rows, 0
    )
    gathered = contract(cycle_gather(own_rows), row_series)
    return gathered.reshape(lax.axis_size("loop"), share_rows, series.shape[0])


def solution(mesh):
    placed = (P("loop", "bulk"),)
    return jax.shard_map(
        on_device, mesh=mesh, in_specs=placed, out_specs=P(None, "bulk", "loop"), check_vma=False
    )
```

profile of v0, /device:TPU:0, one launch (start us, length us, event | category | flops | bytes accessed | tf_op | source)
XLA Modules:
  0.0 174.9 jit_solution(680406850263193112)
XLA Ops:
  6.5 0.0 copy-start
  6.5 0.0 all-gather.4.cloned.1.call-start
  6.5 1.8 %reduce_sum.18 = f32[1056]{0:T(1024)S(1)} reduce(f32[1056,384]{1,0:T(8,128)} %param.1, f32[]{:T(128)} %constant.7.clone.1), dimensions={1}, to_apply=%region_0.0 | reduce | flops 404448 | bytes 1626244 | tf_op jit(solution)/shard_map/reduce_sum | solution.py:29
  8.3 18.3 %psum.14 = f32[1056,1]{0,1:T(1,128)S(1)} all-reduce(f32[1056,1]{0,1:T(1,128)S(1)} %broadcast_in_dim.6), channel_id=1, replica_groups=mesh['loop'=4,'bulk'=8] {'bulk'}, use_global_device_ids=true, to_apply=%region_1.0 | all-reduce | flops 1056 | bytes 8448 | tf_op jit(solution)/shard_map/psum | solution.py:29
  26.7 0.0 copy-done
  26.7 0.4 multiply_reduce_fusion
  27.1 13.9 %psum.15 = f32[1056,1]{0,1:T(1,128)S(1)} all-reduce(f32[1056,1]{0,1:T(1,128)S(1)} %broadcast_in_dim.7), channel_id=1, replica_groups=mesh['loop'=4,'bulk'=8] {'bulk'}, use_global_device_ids=true, to_apply=%region_3.0 | all-reduce | flops 1056 | bytes 8448 | tf_op jit(solution)/shard_map/psum | solution.py:31
  41.1 1.2 multiply_convert_fusion
  42.3 0.0 all-gather.4.cloned.1.call-update
  42.3 0.0 all-gather.6.cloned.1.call-start
  42.4 64.4 %all-gather.4.cloned.1.call-done = bf16[1056,3072]{1,0:T(8,128)(2,1)} async-done(((bf16[1056,384]{1,0:T(8,128)(2,1)}), bf16[1056,3072]{1,0:T(8,128)(2,1)}) %all-gather.4.cloned.1.call-update) | async-done | bytes 6488080 | tf_op jit(solution)/shard_map/all_gather | solution.py:33
  106.8 2.3 %dynamic-slice_bitcast_fusion = bf16[1,132,3072]{2,1,0:T(8,128)(2,1)} fusion(bf16[1056,3072]{1,0:T(8,128)(2,1)} %all-gather.4.cloned.1.call-done, s32[]{:T(128)S(6)} %select_n.3), kind=kLoop, calls=%fused_computation.3 | loop fusion | bytes 1622020
  109.0 0.0 all-gather.6.cloned.1.call-update
  109.1 44.2 %all-gather.6.cloned.1.call-done = bf16[4,132,3072]{2,1,0:T(8,128)(2,1)} async-done(((bf16[1,132,3072]{2,1,0:T(8,128)(2,1)}), bf16[4,132,3072]{2,1,0:T(8,128)(2,1)}) %all-gather.6.cloned.1.call-update) | async-done | bytes 3244048 | tf_op jit(solution)/shard_map/all_gather | solution.py:24
  153.3 2.3 %reshape.5 = bf16[528,3072]{1,0:T(8,128)(2,1)S(1)} reshape(bf16[4,132,3072]{2,1,0:T(8,128)(2,1)} %all-gather.6.cloned.1.call-done) | data formatting | bytes 6488064
  155.6 8.7 %convolution_multiply_fusion = f32[528,1056]{1,0:T(8,128)} fusion(bf16[528,3072]{1,0:T(8,128)(2,1)S(1)} %reshape.5, bf16[1056,3072]{1,0:T(8,128)(2,1)} %all-gather.4.cloned.1.call-done), kind=kOutput, calls=%fused_computation | convolution fusion | flops 3426255360 | bytes 11962368 | tf_op jit(solution)/shard_map/dot_general | solution.py:17
  164.2 1.8 %reshape.3 = f32[4,132,1056]{2,1,0:T(8,128)S(1)} reshape(f32[528,1056]{1,0:T(8,128)} %convolution_multiply_fusion) | data formatting | bytes 4460544 | tf_op jit(solution)/shard_map/reshape | solution.py:38
  166.0 2.1 %copy.4 = f32[4,132,1056]{2,0,1:T(4,128)} copy(f32[4,132,1056]{2,1,0:T(8,128)S(1)} %reshape.3) | data formatting | bytes 4460544 | tf_op jit(solution)/shard_map/reshape | solution.py:38
  (4 shorter events, 0.1 us)
Async XLA Ops:
  6.5 20.2 %copy-start = (f32[1056,384]{1,0:T(8,128)S(1)}, f32[1056,384]{1,0:T(8,128)}, u32[]{:S(2)}) copy-start(f32[1056,384]{1,0:T(8,128)} %param.1) | copy-start | bytes 4866052
  6.5 100.2 %all-gather.4.cloned.1.call-start = ((), (), s32[]{:S(2)}) async-start(), calls=%async_computation | async-start | bytes 7299072 | tf_op jit(solution)/shard_map/all_gather | solution.py:33
  42.3 110.9 %all-gather.6.cloned.1.call-start = ((), (), s32[]{:S(2)}) async-start(), calls=%async_computation.1 | async-start | bytes 4177920 | tf_op jit(solution)/shard_map/all_gather | solution.py:24
Sparse Core Ops, SparseCore 0:
  42.5 64.2 all-gather.3
  109.2 44.0 all-gather.5
where the time goes:
time: 175 us
  waiting for transfers between devices  109 us (62%)
  blocking collectives  32.3 us (18%)
  between operations  13.5 us (8%)
  matrix products  8.65 us (5%)
  local copies, waits for them, and re-layouts  8.41 us (5%)
  other arithmetic  3.46 us (2%)
    all_gather x1, waiting for transfers between devices, on_device(): row_series = lax.all_gather(zscore, 'bulk', axis=1, tiled=True)  64.4 us
    all_gather x1, waiting for transfers between devices, cycle_gather(): return lax.all_gather(own_rows, 'loop', axis=0, tiled=True)  44.2 us
    psum x1, blocking collectives, on_device(): average = lax.psum(jnp.sum(series, axis=1, keepdims=True), 'bulk') / TIME  18.3 us
    psum x1, blocking collectives, on_device(): lax.psum(jnp.sum(centered * centered, axis=1, keepdims=True), 'bulk')  13.9 us
    dot_general x1, matrix products, contract(): lax.dot_general(first_operand, second_operand, (((1,), (1,)), ((), ())),...  8.65 us
    unnamed x4, local copies, waits for them, and re-layouts  4.55 us
    reshape x2, local copies, waits for them, and re-layouts, on_device(): return gathered.reshape(lax.axis_size('loop'), share_rows, series.shape[0])  3.84 us
  transfers between devices with their start and end apart: 2, of which 2 were waited for; matrix products, arithmetic and copies ran while one was open for 0% of the time, Pallas kernels for 0%

commit v1 on v0

v1 whole, which is shorter than its diff:
```python
import functools
import jax
import jax.numpy as jnp
from jax import lax
from jax.experimental import pallas as pl
from jax.experimental.pallas import tpu as pltpu
from jax.sharding import PartitionSpec as P

epsilon = 1e-06
MESH = pl.DeviceIdType.MESH
NT = (((1,), (1,)), ((), ()))
TN = (((0,), (0,)), ((), ()))


def up_to(value, unit):
    return -(-value // unit) * unit


def largest_tile(rows, limit):
    return max(t for t in range(16, limit + 1, 16) if rows % t == 0)


def kernel(L, B, PIECES, x_ref, o_ref, zbuf, shr, acc, cols, stats,
           z_recv, up_send, down_send, mate_send, shr_recv, shr_send, st_recv, st_send):
    R, T = x_ref.shape
    total = T * B
    Q = B // 2
    share = R // B
    SP = shr.shape[2]
    W = min(up_to(share + 15, 16), R)
    PR = R // PIECES
    tile = largest_tile(R, 128)
    l, b = lax.axis_index("loop"), lax.axis_index("bulk")
    q, c = b // 2, b % 2
    mate = q * 2 + (1 - c)

    barrier = pltpu.get_barrier_semaphore()
    for d in range(1, B):
        pl.semaphore_signal(barrier, inc=1, device_id=(l, lax.rem(b + d, B)), device_id_type=MESH)
    for d in range(1, L):
        pl.semaphore_signal(barrier, inc=1, device_id=(lax.rem(l + d, L), b), device_id_type=MESH)

    lane = lax.broadcasted_iota(jnp.int32, (tile, 128), 1)

    @pl.loop(0, R // tile)
    def _(i):
        rows = pl.ds(pl.multiple_of(i * tile, tile), tile)
        v = x_ref[rows, :]
        mean = jnp.sum(v, axis=1, keepdims=True) / T
        dev = v - mean
        m2 = jnp.sum(dev * dev, axis=1, keepdims=True)
        cols[rows, :] = jnp.where(lane == 0, mean, jnp.where(lane == 1, m2, 0.0))

    pick = (lax.broadcasted_iota(jnp.int32, (8, 128), 0)
            == lax.broadcasted_iota(jnp.int32, (8, 128), 1)).astype(jnp.float32)
    line = lax.dot_general(pick, cols[...], NT, precision=lax.Precision.HIGHEST,
                           preferred_element_type=jnp.float32)
    stats[b] = line[:2]

    pl.semaphore_wait(barrier, B - 1 + L - 1)

    def stat_copy(source, peer):
        return pltpu.make_async_remote_copy(
            src_ref=stats.at[source], dst_ref=stats.at[source],
            send_sem=st_send.at[peer], recv_sem=st_recv.at[source],
            device_id=(l, peer), device_id_type=MESH)

    for d in range(1, B):
        stat_copy(b, lax.rem(b + d, B)).start()
    for d in range(1, B):
        other = lax.rem(b + d, B)
        stat_copy(other, other).wait_recv()

    mean = stats[0, 0:1]
    for k in range(1, B):
        mean = mean + stats[k, 0:1]
    mean = mean / B
    square = jnp.zeros_like(mean)
    for k in range(B):
        shift = stats[k, 0:1] - mean
        square = square + (stats[k, 1:2] + T * (shift * shift))
    scale = lax.rsqrt(square / total + epsilon)
    sub = lax.broadcasted_iota(jnp.int32, (8, R), 0)
    both = jnp.where(sub == 0, mean, jnp.where(sub == 1, scale, 0.0))
    cols[...] = lax.dot_general(both, pick, TN, precision=lax.Precision.HIGHEST,
                                preferred_element_type=jnp.float32)

    @pl.loop(0, R // tile)
    def _(i):
        rows = pl.ds(pl.multiple_of(i * tile, tile), tile)
        z = (x_ref[rows, :] - cols[rows, 0:1]) * cols[rows, 1:2]
        zbuf[b, rows, :] = z.astype(jnp.bfloat16)

    def piece_copy(k, piece, send_sem, peer):
        part = zbuf.at[k, pl.ds(pl.multiple_of(piece * PR, 16), PR), :]
        return pltpu.make_async_remote_copy(
            src_ref=part, dst_ref=part, send_sem=send_sem.at[k, piece],
            recv_sem=z_recv.at[k, piece], device_id=(l, peer), device_id_type=MESH)

    def share_copy(k, block, peer):
        return pltpu.make_async_remote_copy(
            src_ref=shr.at[k, block], dst_ref=shr.at[k, block], send_sem=shr_send.at[k, peer],
            recv_sem=shr_recv.at[k, block], device_id=(peer, b), device_id_type=MESH)

    has_up, has_down = q + 1 < Q, q >= 1
    start = b * share
    first = pl.multiple_of(jnp.minimum(start // 16 * 16, R - W), 16)
    need_below = PIECES - 1 - first // PR
    need_above = (first + W - 1) // PR

    def extract(k):
        window = zbuf[k, pl.ds(first, W), :]
        hot = (lax.broadcasted_iota(jnp.int32, (SP, W), 1)
               == lax.broadcasted_iota(jnp.int32, (SP, W), 0) + (start - first))
        inside = lax.broadcasted_iota(jnp.int32, (SP, W), 0) < share
        hot = jnp.where(hot & inside, 1.0, 0.0).astype(jnp.bfloat16)
        rows = lax.dot_general(hot, window, (((1,), (0,)), ((), ())),
                               preferred_element_type=jnp.float32)
        shr[k, l] = rows.astype(jnp.bfloat16)
        for d in range(1, L):
            share_copy(k, l, lax.rem(l + d, L)).start()

    def multiply(k):
        for d in range(1, L):
            other = lax.rem(l + d, L)
            share_copy(k, other, other).wait_recv()
        a = shr[k].reshape(L * SP, T)
        acc[...] += lax.dot_general(a, zbuf[k], NT, preferred_element_type=jnp.float32)

    def multiply_step(s):
        @pl.loop(0, 4)
        def _(n):
            sign = 1 - 2 * (n // 2)
            place = q - sign * s
            k = place * 2 + n % 2

            @pl.when((place >= 0) & (place < Q) & ((s > 0) | (n < 2)))
            def _():
                multiply(k)

    @pl.loop(0, PIECES)
    def _(i):
        @pl.when(has_up)
        def _():
            piece_copy(b, PIECES - 1 - i, up_send, b + 2).start()

        @pl.when(has_down)
        def _():
            piece_copy(b, i, down_send, b - 2).start()

    @pl.loop(0, PIECES)
    def _(i):
        piece_copy(b, i, mate_send, mate).start()

    acc[...] = jnp.zeros_like(acc)
    extract(b)

    @pl.loop(0, PIECES)
    def _(i):
        piece_copy(mate, i, mate_send, mate).wait_recv()

    extract(mate)

    @pl.loop(1, Q)
    def _(s):
        below, above = b - 2 * s, b + 2 * s
        from_below, from_above = q - s >= 0, q + s < Q

        @pl.loop(0, PIECES)
        def _(i):
            down_piece = PIECES - 1 - i

            @pl.when(from_below)
            def _():
                piece_copy(below, down_piece, up_send, b).wait_recv()

                @pl.when(has_up)
                def _():
                    piece_copy(below, down_piece, up_send, b + 2).start()
                piece_copy(below, down_piece, mate_send, mate).start()

            @pl.when(from_above)
            def _():
                piece_copy(above, i, down_send, b).wait_recv()

                @pl.when(has_down)
                def _():
                    piece_copy(above, i, down_send, b - 2).start()
                piece_copy(above, i, mate_send, mate).start()

            @pl.when(from_below & (i == need_below))
            def _():
                extract(below)

            @pl.when(from_above & (i == need_above))
            def _():
                extract(above)

            @pl.when(from_below)
            def _():
                piece_copy(mate - 2 * s, down_piece, mate_send, mate).wait_recv()

                @pl.when(i == need_below)
                def _():
                    extract(mate - 2 * s)

            @pl.when(from_above)
            def _():
                piece_copy(mate + 2 * s, i, mate_send, mate).wait_recv()

                @pl.when(i == need_above)
                def _():
                    extract(mate + 2 * s)

            @pl.when(i == 0)
            def _():
                multiply_step(s - 1)

    multiply_step(Q - 1)

    for j in range(L):
        o_ref[j] = acc[j * SP:j * SP + share, :] / total

    for d in range(1, B):
        other = lax.rem(b + d, B)
        stat_copy(b, other).wait_send()

    @pl.loop(0, Q)
    def _(s):
        below, above = b - 2 * s, b + 2 * s
        from_below, from_above = q - s >= 0, q + s < Q

        @pl.loop(0, PIECES)
        def _(i):
            @pl.when(from_below & has_up)
            def _():
                piece_copy(below, i, up_send, b + 2).wait_send()

            @pl.when(from_above & has_down)
            def _():
                piece_copy(above, i, down_send, b - 2).wait_send()

            @pl.when(from_below)
            def _():
                piece_copy(below, i, mate_send, mate).wait_send()

            @pl.when(from_above & (s > 0))
            def _():
                piece_copy(above, i, mate_send, mate).wait_send()

    @pl.loop(0, B)
    def _(k):
        for d in range(1, L):
            other = lax.rem(l + d, L)
            share_copy(k, l, other).wait_send()


def solution(mesh):
    L, B = mesh.shape["loop"], mesh.shape["bulk"]

    def on_device(series):
        R, T = series.shape
        share = R // B
        SP = up_to(share, 16)
        pieces = 3
        vmem = pl.BlockSpec(memory_space=pltpu.VMEM)
        dma = pltpu.SemaphoreType.DMA
        return pl.pallas_call(
            functools.partial(kernel, L, B, pieces),
            out_shape=jax.ShapeDtypeStruct((L, share, R), jnp.float32),
            in_specs=[vmem],
            out_specs=vmem,
            scratch_shapes=[
                pltpu.VMEM((B, R, T), jnp.bfloat16),
                pltpu.VMEM((B, L, SP, T), jnp.bfloat16),
                pltpu.VMEM((L * SP, R), jnp.float32),
                pltpu.VMEM((R, 128), jnp.float32),
                pltpu.VMEM((B, 2, R), jnp.float32),
                dma((B, pieces)), dma((B, pieces)), dma((B, pieces)), dma((B, pieces)),
                dma((B, L)), dma((B, L)), dma((B,)), dma((B,)),
            ],
            compiler_params=pltpu.CompilerParams(
                collective_id=0, has_side_effects=True, vmem_limit_bytes=56 * 1024 * 1024),
        )(series)

    return jax.shard_map(
        on_device, mesh=mesh, in_specs=(P("loop", "bulk"),),
        out_specs=P(None, "bulk", "loop"), check_vma=False)
```

time: 175 us -> 76.8 us (0.44)
  waiting for transfers between devices: 109 us -> 0 us
  Pallas kernels: 0 us -> 72.4 us
  blocking collectives: 32.3 us -> 0 us
  between operations: 13.5 us -> 0.01 us
  matrix products: 8.65 us -> 0 us
  local copies, waits for them, and re-layouts: 8.41 us -> 3.76 us
  other arithmetic: 3.46 us -> 0 us
    all_gather x2 -> x0, waiting for transfers between devices: 109 us -> none  [the longest x1 64.4 us: on_device(): row_series = lax.all_gather(zscore, 'bulk', axis=1, tiled=True)]
    pallas_call x0 -> x1, Pallas kernels: none -> 72.4 us  [on_device(): pl.pallas_call(functools.partial(kernel, L, B, pieces), out_shape=jax.Sha...]
    psum x2 -> x0, blocking collectives: 32.3 us -> none  [the longest x1 18.3 us: on_device(): average = lax.psum(jnp.sum(series, axis=1, keepdims=True), 'bulk') / TIME]
    dot_general x1 -> x0, matrix products: 8.65 us -> none  [contract(): lax.dot_general(first_operand, second_operand, (((1,), (1,)), ((), ())),...]
    unnamed x4 -> x0, local copies, waits for them, and re-layouts: 4.55 us -> none
    reshape x2 -> x0, local copies, waits for them, and re-layouts: 3.84 us -> none  [on_device(): return gathered.reshape(lax.axis_size('loop'), share_rows, series.shape[0])]
    pallas_call x0 -> x1, local copies, waits for them, and re-layouts: none -> 3.76 us  [on_device(): pl.pallas_call(functools.partial(kernel, L, B, pieces), out_shape=jax.Sha...]
    reduce_sum x2 -> x0, other arithmetic: 2.18 us -> none  [the longest x1 1.78 us: on_device(): average = lax.psum(jnp.sum(series, axis=1, keepdims=True), 'bulk') / TIME]
  transfers between devices with their start and end apart: 2 -> 0, of which waited for: 2 -> 0; matrix products, arithmetic and copies ran while one was open for 0% -> 0% of each run, Pallas kernels for 0% -> 0%
where the time goes in v1:
time: 76.8 us; the launch traced here: 76.2 us
  Pallas kernels  72.4 us (94%)
  local copies, waits for them, and re-layouts  3.76 us (5%)
    pallas_call x1, Pallas kernels, on_device(): pl.pallas_call(functools.partial(kernel, L, B, pieces), out_shape=jax.Sha...  72.4 us
    pallas_call x1, local copies, waits for them, and re-layouts, on_device(): pl.pallas_call(functools.partial(kernel, L, B, pieces), out_shape=jax.Sha...  3.76 us

profile of v1, /device:TPU:0, one launch (start us, length us, event | category | flops | bytes accessed | tf_op | source)
XLA Modules:
  0.0 76.2 jit_solution(10829517958671756849)
XLA Ops:
  0.0 72.4 %shard_map.17 = f32[4,132,1056]{2,1,0:T(8,128)} custom-call(f32[1056,384]{1,0:T(8,128)} %x_ref.1), custom_call_target="tpu_custom_call" | custom-call | tf_op jit(solution)/shard_map/pallas_call | solution.py:268
  72.4 3.8 %copy.2 = f32[4,132,1056]{2,0,1:T(4,128)} copy(f32[4,132,1056]{2,1,0:T(8,128)} %shard_map.17) | data formatting | bytes 4460544 | tf_op jit(solution)/shard_map/pallas_call | solution.py:268

commit v2 on v1

v2 whole, which is shorter than its diff:
```python
import functools
import jax
import jax.numpy as jnp
from jax import lax
from jax.experimental import pallas as pl
from jax.experimental.pallas import tpu as pltpu
from jax.sharding import PartitionSpec as P

epsilon = 1e-06
MESH = pl.DeviceIdType.MESH
NT = (((1,), (1,)), ((), ()))
TN = (((0,), (0,)), ((), ()))


def up_to(value, unit):
    return -(-value // unit) * unit


def largest_tile(rows, limit):
    return max(t for t in range(16, limit + 1, 16) if rows % t == 0)


def kernel(L, B, PIECES, x_hbm, o_ref, zbuf, shr, acc, cols, stats, x_ref,
           z_recv, up_send, down_send, mate_send, shr_recv, shr_send, st_recv, st_send, x_sem):
    R, T = x_hbm.shape
    total = T * B
    Q = B // 2
    share = R // B
    SP = shr.shape[2]
    W = min(up_to(share + 15, 16), R)
    bounds = [up_to(R * i // PIECES, 128) for i in range(PIECES)] + [R]
    tile = largest_tile(R, 128)
    l, b = lax.axis_index("loop"), lax.axis_index("bulk")
    q, c = b // 2, b % 2
    mate = q * 2 + (1 - c)

    barrier = pltpu.get_barrier_semaphore()
    for d in range(1, B):
        pl.semaphore_signal(barrier, inc=1, device_id=(l, lax.rem(b + d, B)), device_id_type=MESH)
    for d in range(1, L):
        pl.semaphore_signal(barrier, inc=1, device_id=(lax.rem(l + d, L), b), device_id_type=MESH)

    def load(i):
        rows = pl.ds(pl.multiple_of(i * tile, tile), tile)
        return pltpu.make_async_copy(x_hbm.at[rows, :], x_ref.at[rows, :], x_sem.at[i])

    @pl.loop(0, R // tile)
    def _(i):
        load(i).start()

    lane = lax.broadcasted_iota(jnp.int32, (tile, 128), 1)

    @pl.loop(0, R // tile)
    def _(i):
        rows = pl.ds(pl.multiple_of(i * tile, tile), tile)
        load(i).wait()
        v = x_ref[rows, :]
        mean = jnp.sum(v, axis=1, keepdims=True) / T
        dev = v - mean
        m2 = jnp.sum(dev * dev, axis=1, keepdims=True)
        cols[rows, :] = jnp.where(lane == 0, mean, jnp.where(lane == 1, m2, 0.0))

    pick = (lax.broadcasted_iota(jnp.int32, (8, 128), 0)
            == lax.broadcasted_iota(jnp.int32, (8, 128), 1)).astype(jnp.float32)
    line = lax.dot_general(pick, cols[...], NT, precision=lax.Precision.HIGHEST,
                           preferred_element_type=jnp.float32)
    stats[b] = line[:2]

    pl.semaphore_wait(barrier, B - 1 + L - 1)

    def stat_copy(source, peer):
        return pltpu.make_async_remote_copy(
            src_ref=stats.at[source], dst_ref=stats.at[source],
            send_sem=st_send.at[peer], recv_sem=st_recv.at[source],
            device_id=(l, peer), device_id_type=MESH)

    for d in range(1, B):
        stat_copy(b, lax.rem(b + d, B)).start()
    for d in range(1, B):
        other = lax.rem(b + d, B)
        stat_copy(other, other).wait_recv()

    mean = stats[0, 0:1]
    for k in range(1, B):
        mean = mean + stats[k, 0:1]
    mean = mean / B
    square = jnp.zeros_like(mean)
    for k in range(B):
        shift = stats[k, 0:1] - mean
        square = square + (stats[k, 1:2] + T * (shift * shift))
    scale = lax.rsqrt(square / total + epsilon)
    sub = lax.broadcasted_iota(jnp.int32, (8, R), 0)
    both = jnp.where(sub == 0, mean, jnp.where(sub == 1, scale, 0.0))
    cols[...] = lax.dot_general(both, pick, TN, precision=lax.Precision.HIGHEST,
                                preferred_element_type=jnp.float32)

    def normalise(piece):
        size = bounds[piece + 1] - bounds[piece]
        step = largest_tile(size, 128)

        @pl.loop(0, size // step)
        def _(i):
            rows = pl.ds(pl.multiple_of(bounds[piece] + i * step, 16), step)
            z = (x_ref[rows, :] - cols[rows, 0:1]) * cols[rows, 1:2]
            zbuf[b, rows, :] = z.astype(jnp.bfloat16)

    def piece_copy(k, piece, send_sem, peer):
        part = zbuf.at[k, pl.ds(bounds[piece], bounds[piece + 1] - bounds[piece]), :]
        return pltpu.make_async_remote_copy(
            src_ref=part, dst_ref=part, send_sem=send_sem.at[k, piece],
            recv_sem=z_recv.at[k, piece], device_id=(l, peer), device_id_type=MESH)

    def share_copy(k, block, peer):
        return pltpu.make_async_remote_copy(
            src_ref=shr.at[k, block], dst_ref=shr.at[k, block], send_sem=shr_send.at[k, peer],
            recv_sem=shr_recv.at[k, block], device_id=(peer, b), device_id_type=MESH)

    has_up, has_down = q + 1 < Q, q >= 1
    start = b * share
    first = pl.multiple_of(jnp.minimum(start // 16 * 16, R - W), 16)
    need_below = PIECES - 1 - sum((first >= x).astype(jnp.int32) for x in bounds[1:-1])
    need_above = sum((first + W > x).astype(jnp.int32) for x in bounds[1:-1])

    def extract(k):
        window = zbuf[k, pl.ds(first, W), :]
        hot = (lax.broadcasted_iota(jnp.int32, (SP, W), 1)
               == lax.broadcasted_iota(jnp.int32, (SP, W), 0) + (start - first))
        inside = lax.broadcasted_iota(jnp.int32, (SP, W), 0) < share
        hot = jnp.where(hot & inside, 1.0, 0.0).astype(jnp.bfloat16)
        rows = lax.dot_general(hot, window, (((1,), (0,)), ((), ())),
                               preferred_element_type=jnp.float32)
        shr[k, l] = rows.astype(jnp.bfloat16)
        for d in range(1, L):
            share_copy(k, l, lax.rem(l + d, L)).start()

    def wait_shares(place):
        for core in range(2):
            k = place * 2 + core
            for d in range(1, L):
                other = lax.rem(l + d, L)
                share_copy(k, other, other).wait_recv()

    def multiply(place):
        part = None
        wait_shares(place)
        for core in range(2):
            k = place * 2 + core
            a = shr[k].reshape(L * SP, T)
            term = lax.dot_general(a, zbuf[k], NT, preferred_element_type=jnp.float32)
            part = term if part is None else part + term
        acc[...] += part

    def multiply_step(s):
        @pl.loop(0, 2)
        def _(n):
            place = q - (1 - 2 * n) * s

            @pl.when((place >= 0) & (place < Q) & ((s > 0) | (n < 1)))
            def _():
                multiply(place)

    done = set()

    def ready(piece):
        if piece not in done:
            done.add(piece)
            normalise(piece)

    for i in range(PIECES):
        ready(PIECES - 1 - i)

        @pl.when(has_up)
        def _():
            piece_copy(b, PIECES - 1 - i, up_send, b + 2).start()

        ready(i)

        @pl.when(has_down)
        def _():
            piece_copy(b, i, down_send, b - 2).start()

    for i in range(PIECES):
        piece_copy(b, i, mate_send, mate).start()

    acc[...] = jnp.zeros_like(acc)
    extract(b)

    for i in range(PIECES):
        piece_copy(mate, i, mate_send, mate).wait_recv()

    extract(mate)

    def arrive(s, i, between=None):
        below, above = b - 2 * s, b + 2 * s
        from_below, from_above = q - s >= 0, q + s < Q
        down_piece = PIECES - 1 - i

        @pl.when(from_below)
        def _():
            piece_copy(below, down_piece, up_send, b).wait_recv()

            @pl.when(has_up)
            def _():
                piece_copy(below, down_piece, up_send, b + 2).start()
            piece_copy(below, down_piece, mate_send, mate).start()

        @pl.when(from_above)
        def _():
            piece_copy(above, i, down_send, b).wait_recv()

            @pl.when(has_down)
            def _():
                piece_copy(above, i, down_send, b - 2).start()
            piece_copy(above, i, mate_send, mate).start()

        @pl.when(from_below & (i == need_below))
        def _():
            extract(below)

        @pl.when(from_above & (i == need_above))
        def _():
            extract(above)

        if between is not None:
            between()

        @pl.when(from_below)
        def _():
            piece_copy(mate - 2 * s, down_piece, mate_send, mate).wait_recv()

            @pl.when(i == need_below)
            def _():
                extract(mate - 2 * s)

        @pl.when(from_above)
        def _():
            piece_copy(mate + 2 * s, i, mate_send, mate).wait_recv()

            @pl.when(i == need_above)
            def _():
                extract(mate + 2 * s)

        if i == 0:
            multiply_step(s - 1)

    def finish(piece, place):
        lo, hi = bounds[piece], bounds[piece + 1]
        part = acc[:, lo:hi]
        if place is not None:
            for core in range(2):
                k = place * 2 + core
                a = shr[k].reshape(L * SP, T)
                part = part + lax.dot_general(a, zbuf[k, lo:hi, :], NT,
                                              preferred_element_type=jnp.float32)
        part = part / total
        for j in range(L):
            o_ref[:, j, lo:hi] = part[j * SP:j * SP + share]

    @pl.loop(1, Q - 1)
    def _(s):
        for i in range(PIECES):
            arrive(s, i)

    def finish_ends(steps):
        for end, place in ((Q - 1, 0), (0, Q - 1)):
            @pl.when(q == end)
            def _():
                for i in steps:
                    finish(PIECES - 1 - i if end else i, place)

    def finish_early():
        for end, place in ((Q - 1, 0), (0, Q - 1)):
            @pl.when(q == end)
            def _():
                wait_shares(place)

        finish_ends(range(PIECES - 1))

    for i in range(PIECES):
        arrive(Q - 1, i, finish_early if i == PIECES - 1 else None)
    finish_ends([PIECES - 1])

    @pl.when((q > 0) & (q < Q - 1))
    def _():
        for i in range(PIECES):
            finish(i, None)

    for d in range(1, B):
        other = lax.rem(b + d, B)
        stat_copy(b, other).wait_send()

    @pl.loop(0, Q)
    def _(s):
        below, above = b - 2 * s, b + 2 * s
        from_below, from_above = q - s >= 0, q + s < Q

        for i in range(PIECES):
            @pl.when(from_below & has_up)
            def _():
                piece_copy(below, i, up_send, b + 2).wait_send()

            @pl.when(from_above & has_down)
            def _():
                piece_copy(above, i, down_send, b - 2).wait_send()

            @pl.when(from_below)
            def _():
                piece_copy(below, i, mate_send, mate).wait_send()

            @pl.when(from_above & (s > 0))
            def _():
                piece_copy(above, i, mate_send, mate).wait_send()

    @pl.loop(0, B)
    def _(k):
        for d in range(1, L):
            other = lax.rem(l + d, L)
            share_copy(k, l, other).wait_send()


def solution(mesh):
    L, B = mesh.shape["loop"], mesh.shape["bulk"]

    def on_device(series):
        R, T = series.shape
        share = R // B
        SP = up_to(share, 16)
        pieces = 3
        vmem = pl.BlockSpec(memory_space=pltpu.VMEM)
        dma = pltpu.SemaphoreType.DMA
        return pl.pallas_call(
            functools.partial(kernel, L, B, pieces),
            out_shape=jax.ShapeDtypeStruct((share, L, R), jnp.float32),
            in_specs=[pl.BlockSpec(memory_space=pltpu.HBM)],
            out_specs=vmem,
            scratch_shapes=[
                pltpu.VMEM((B, R, T), jnp.bfloat16),
                pltpu.VMEM((B, L, SP, T), jnp.bfloat16),
                pltpu.VMEM((L * SP, R), jnp.float32),
                pltpu.VMEM((R, 128), jnp.float32),
                pltpu.VMEM((B, 2, R), jnp.float32),
                pltpu.VMEM((R, T), jnp.float32),
                dma((B, pieces)), dma((B, pieces)), dma((B, pieces)), dma((B, pieces)),
                dma((B, L)), dma((B, L)), dma((B,)), dma((B,)), dma((R // largest_tile(R, 128),)),
            ],
            compiler_params=pltpu.CompilerParams(
                collective_id=0, has_side_effects=True, vmem_limit_bytes=26 * 1024 * 1024),
        )(pltpu.with_memory_space_constraint(series, pltpu.HBM)).transpose(1, 0, 2)

    return jax.shard_map(
        on_device, mesh=mesh, in_specs=(P("loop", "bulk"),),
        out_specs=P(None, "bulk", "loop"), check_vma=False)
```

time: 76.8 us -> 71.8 us (0.935)
  local copies, waits for them, and re-layouts: 3.76 us -> 1.43 us
  Pallas kernels: 72.4 us -> 70.2 us
    pallas_call x1 -> x0, local copies, waits for them, and re-layouts: 3.76 us -> none  [on_device(): pl.pallas_call(functools.partial(kernel, L, B, pieces), out_shape=jax.Sha...]
    pallas_call x1, Pallas kernels: 72.4 us -> 70.2 us  [on_device(): pl.pallas_call(functools.partial(kernel, L, B, pieces), out_shape=jax.Sha...]
    unnamed x0 -> x1, local copies, waits for them, and re-layouts: none -> 1.43 us
where the time goes in v2:
time: 71.8 us; the launch traced here: 71.7 us
  Pallas kernels  70.2 us (98%)
  local copies, waits for them, and re-layouts  1.43 us (2%)
    pallas_call x1, Pallas kernels, on_device(): pl.pallas_call(functools.partial(kernel, L, B, pieces), out_shape=jax.Sha...  70.2 us

profile of v2, /device:TPU:0, one launch (start us, length us, event | category | flops | bytes accessed | tf_op | source)
XLA Modules:
  0.0 71.7 jit_solution(6065414231796189002)
XLA Ops:
  0.0 70.2 %shard_map.17 = f32[132,4,1056]{2,1,0:T(4,128)S(1)} custom-call(f32[1056,384]{1,0:T(8,128)} %x_hbm.1), custom_call_target="tpu_custom_call" | custom-call | tf_op jit(solution)/shard_map/pallas_call | solution.py:331
  70.2 1.4 %copy.3 = f32[4,132,1056]{2,0,1:T(4,128)} copy(f32[4,132,1056]{2,0,1:T(4,128)S(1)} %bitcast.1) | data formatting | bytes 4460544

commit v3 on v2

--- a/solution.py
+++ b/solution.py
@@ -34,19 +34,30 @@
     q, c = b // 2, b % 2
     mate = q * 2 + (1 - c)
 
+    def load(i):
+        rows = pl.ds(pl.multiple_of(i * tile, tile), tile)
+        return pltpu.make_async_copy(x_hbm.at[rows, :], x_ref.at[rows, :], x_sem.at[i])
+
+    @pl.loop(0, R // tile)
+    def _(i):
+        load(i).start()
+
     barrier = pltpu.get_barrier_semaphore()
+    outer = (q < Q // 4) | ((q >= Q // 2) & (q < Q - Q // 4))
+    sign = jnp.where(outer, -1, 1)
+
+    def far_first(act):
+        for e in range(B):
+            peer = lax.rem(2 * B - 1 - b + sign * e, B)
+
+            @pl.when(peer != b)
+            def _():
+                act(peer)
+
     for d in range(1, B):
         pl.semaphore_signal(barrier, inc=1, device_id=(l, lax.rem(b + d, B)), device_id_type=MESH)
     for d in range(1, L):
         pl.semaphore_signal(barrier, inc=1, device_id=(lax.rem(l + d, L), b), device_id_type=MESH)
-
-    def load(i):
-        rows = pl.ds(pl.multiple_of(i * tile, tile), tile)
-        return pltpu.make_async_copy(x_hbm.at[rows, :], x_ref.at[rows, :], x_sem.at[i])
-
-    @pl.loop(0, R // tile)
-    def _(i):
-        load(i).start()
 
     lane = lax.broadcasted_iota(jnp.int32, (tile, 128), 1)
 
@@ -74,8 +85,7 @@
             send_sem=st_send.at[peer], recv_sem=st_recv.at[source],
             device_id=(l, peer), device_id_type=MESH)
 
-    for d in range(1, B):
-        stat_copy(b, lax.rem(b + d, B)).start()
+    far_first(lambda peer: stat_copy(b, peer).start())
     for d in range(1, B):
         other = lax.rem(b + d, B)
         stat_copy(other, other).wait_recv()
@@ -182,8 +192,8 @@
     for i in range(PIECES):
         piece_copy(b, i, mate_send, mate).start()
 
+    extract(b)
     acc[...] = jnp.zeros_like(acc)
-    extract(b)
 
     for i in range(PIECES):
         piece_copy(mate, i, mate_send, mate).wait_recv()
@@ -252,7 +262,7 @@
                 a = shr[k].reshape(L * SP, T)
                 part = part + lax.dot_general(a, zbuf[k, lo:hi, :], NT,
                                               preferred_element_type=jnp.float32)
-        part = part / total
+        part = part * (1.0 / total)
         for j in range(L):
             o_ref[:, j, lo:hi] = part[j * SP:j * SP + share]
 

time: 71.8 us -> 71.7 us (level)
  no operation moved by 1% of the time
where the time goes in v3:
time: 71.7 us; the launch traced here: 71.6 us
  Pallas kernels  70.2 us (98%)
  local copies, waits for them, and re-layouts  1.43 us (2%)
    pallas_call x1, Pallas kernels, on_device(): pl.pallas_call(functools.partial(kernel, L, B, pieces), out_shape=jax.Sha...  70.2 us

profile of v3, /device:TPU:0, one launch (start us, length us, event | category | flops | bytes accessed | tf_op | source)
XLA Modules:
  0.0 71.6 jit_solution(5131459801534626148)
XLA Ops:
  0.0 70.2 %shard_map.17 = f32[132,4,1056]{2,1,0:T(4,128)S(1)} custom-call(f32[1056,384]{1,0:T(8,128)} %x_hbm.1), custom_call_target="tpu_custom_call" | custom-call | tf_op jit(solution)/shard_map/pallas_call | solution.py:341
  70.2 1.4 %copy.3 = f32[4,132,1056]{2,0,1:T(4,128)} copy(f32[4,132,1056]{2,0,1:T(4,128)S(1)} %bitcast.1) | data formatting | bytes 4460544

commit v4 on v2

--- a/solution.py
+++ b/solution.py
@@ -159,25 +159,33 @@
             def _():
                 multiply(place)
 
-    done = set()
-
-    def ready(piece):
-        if piece not in done:
-            done.add(piece)
-            normalise(piece)
-
-    for i in range(PIECES):
-        ready(PIECES - 1 - i)
-
-        @pl.when(has_up)
-        def _():
-            piece_copy(b, PIECES - 1 - i, up_send, b + 2).start()
-
-        ready(i)
-
-        @pl.when(has_down)
-        def _():
-            piece_copy(b, i, down_send, b - 2).start()
+    def send_own(up_first):
+        done = set()
+
+        def send(up, i):
+            piece = PIECES - 1 - i if up else i
+            if piece not in done:
+                done.add(piece)
+                normalise(piece)
+
+            @pl.when(has_up if up else has_down)
+            def _():
+                if up:
+                    piece_copy(b, piece, up_send, b + 2).start()
+                else:
+                    piece_copy(b, piece, down_send, b - 2).start()
+
+        for i in range(PIECES):
+            send(up_first, i)
+            send(not up_first, i)
+
+    @pl.when(q >= Q // 2)
+    def _():
+        send_own(True)
+
+    @pl.when(q < Q // 2)
+    def _():
+        send_own(False)
 
     for i in range(PIECES):
         piece_copy(b, i, mate_send, mate).start()

time: 71.8 us -> 71.5 us (level)
  no operation moved by 1% of the time
where the time goes in v4:
time: 71.5 us; the launch traced here: 71.4 us
  Pallas kernels  70 us (98%)
  local copies, waits for them, and re-layouts  1.43 us (2%)
    pallas_call x1, Pallas kernels, on_device(): pl.pallas_call(functools.partial(kernel, L, B, pieces), out_shape=jax.Sha...  70 us
    unnamed x1, local copies, waits for them, and re-layouts  1.43 us

profile of v4, /device:TPU:0, one launch (start us, length us, event | category | flops | bytes accessed | tf_op | source)
XLA Modules:
  0.0 71.4 jit_solution(7071849981405193399)
XLA Ops:
  0.0 70.0 %shard_map.17 = f32[132,4,1056]{2,1,0:T(4,128)S(1)} custom-call(f32[1056,384]{1,0:T(8,128)} %x_hbm.1), custom_call_target="tpu_custom_call" | custom-call | tf_op jit(solution)/shard_map/pallas_call | solution.py:339
  70.0 1.4 %copy.3 = f32[4,132,1056]{2,0,1:T(4,128)} copy(f32[4,132,1056]{2,0,1:T(4,128)S(1)} %bitcast.1) | data formatting | bytes 4460544
